TPU v7x, 32 devices: a whole 2x2x4 slice. The times are simulated.
32 devices in a mesh: groups: 2 (over y), chol: 4 (over z), occ: 4 (over x, core).
Axes of the slice: x: 2, y: 2, z: 4, core: 2. Of those that a mesh axis runs over, the one named last changes fastest.
Arguments:
- chol_rot: bfloat16 [96, 256, 2048], P(('groups', 'chol'), 'occ'), parts along dimension 0, may hold values from -0.1875 to 0.1875
- green: bfloat16 [4, 256, 2048], P('groups', 'occ', 'chol'), parts along dimension 0, may hold values from -6 to 6
Outputs:
- gradient: float32 [256, 4, 2048], P('occ', 'groups', 'chol'), parts along dimension 1
There are 2 independent parts, one for each index of `groups`. A program takes and returns all parts, laid end to end along the dimension named above; each array names one. Nothing has to cross between parts.
All inputs are finite; a program needn't handle non-finite values.
Results may differ from a plain program's by a relative error of at most 0.0085.
Values may be sent and summed in bfloat16 or wider, within the bound.
No kernel may reach another device: no remote copies, remote signals or barrier semaphores. Data moves between devices by JAX's collectives and lax.ppermute only.
A program may use at most 64 MiB of HBM per device.

v0:
```python
import math
import jax
import jax.numpy as jnp
from jax import lax
from jax.sharding import PartitionSpec as P


def local(chol_rot, green):
    chol_loc, occ_loc, orbitals = chol_rot.shape
    walkers = green.shape[0]
    occupied = occ_loc * lax.axis_size("occ")
    nvec = chol_loc * lax.axis_size("chol")
    factor = -math.sqrt(orbitals / (nvec * occupied))
    vec_mat = chol_rot.reshape(chol_loc * occ_loc, orbitals)
    green_all = lax.all_gather(green, "occ", axis=1, tiled=True)
    piece = lax.all_gather(green_all, "chol", axis=2, tiled=True)
    flat = piece.reshape(-1, piece.shape[2])
    pair_sum = jnp.dot(vec_mat, flat.T, preferred_element_type=jnp.float32)
    pairs = pair_sum.astype(jnp.bfloat16).reshape(chol_loc, occ_loc, walkers, occupied)
    swapped = lax.all_to_all(pairs, "occ", split_axis=3, concat_axis=1, tiled=True)
    occ_summed = lax.psum_scatter(
        jnp.einsum("gjwi,gip->jwp", swapped, chol_rot, preferred_element_type=jnp.float32).astype(
            jnp.bfloat16
        ),
        "occ",
        scatter_dimension=0,
        tiled=True,
    ).astype(jnp.float32)
    summed = lax.psum_scatter(occ_summed, "chol", scatter_dimension=2, tiled=True)
    return summed * factor


def solution(mesh):
    return jax.shard_map(
        local,
        mesh=mesh,
        in_specs=(P(("groups", "chol"), "occ", None), P("groups", "occ", "chol")),
        out_specs=P("occ", "groups", "chol"),
        check_vma=False,
    )
```

profile of v0, /device:TPU:0, one launch (start us, length us, event | category | flops | bytes accessed | tf_op | source)
XLA Modules:
  0.0 178.3 jit_solution(8074986663680790082)
XLA Ops:
  6.5 0.0 copy-start
  6.5 0.0 all-gather.2.cloned.1.call-start
  6.5 10.5 %all_gather.6 = bf16[2,256,512]{2,1,0:T(8,128)(2,1)} all-gather(bf16[2,64,512]{2,1,0:T(8,128)(2,1)} %param.3), channel_id=1, replica_groups=mesh['groups'=2,'chol'=4,'occ'=4] {'occ'}, dimensions={1}, use_global_device_ids=true | all-gather | bytes 655360 | tf_op jit(solution)/shard_map/all_gather | solution.py:15
  17.0 0.0 all-gather.2.cloned.1.call-update
  17.0 0.0 reduce-scatter.3.cloned.1.call-start
  17.1 46.1 %all-gather.2.cloned.1.call-done = bf16[2,256,2048]{2,1,0:T(8,128)(2,1)} async-done(((bf16[2,256,512]{2,1,0:T(8,128)(2,1)}), bf16[2,256,2048]{2,1,0:T(8,128)(2,1)}) %all-gather.2.cloned.1.call-update) | async-done | bytes 2097168 | tf_op jit(solution)/shard_map/all_gather | solution.py:16
  63.2 0.0 copy-done
  63.2 4.3 %convolution_convert_fusion = bf16[768,512]{1,0:T(8,128)(2,1)} fusion(bf16[768,2048]{1,0:T(8,128)(2,1)S(1)} %bitcast.19, bf16[512,2048]{1,0:T(8,128)(2,1)} %bitcast.23), kind=kOutput, calls=%fused_computation.3 | convolution fusion | flops 1611005952 | bytes 6029312 | tf_op jit(solution)/shard_map/dot_general | solution.py:18
  67.5 2.9 %reshape.11 = bf16[12,64,2,256]{3,2,1,0:T(2,128)(2,1)} reshape(bf16[768,512]{1,0:T(8,128)(2,1)} %convolution_convert_fusion) | data formatting | bytes 1572864 | tf_op jit(solution)/shard_map/reshape | solution.py:19
  70.4 5.0 %copy.8 = bf16[12,64,2,256]{1,2,0,3:T(2,128)(2,1)} copy(bf16[12,64,2,256]{3,2,1,0:T(2,128)(2,1)} %reshape.11) | data formatting | bytes 1572864 | tf_op jit(solution)/shard_map/reshape | solution.py:19
  75.4 4.0 %reshape.14 = bf16[4,2,49152]{2,1,0:T(2,128)(2,1)} reshape(bf16[256,12,2,64]{3,2,1,0:T(2,128)(2,1)} %bitcast.20) | data formatting | bytes 1572864
  79.5 15.9 %all_to_all.18 = bf16[4,2,49152]{2,1,0:T(2,128)(2,1)} all-to-all(bf16[4,2,49152]{2,1,0:T(2,128)(2,1)} %reshape.14), channel_id=1, replica_groups=mesh['groups'=2,'chol'=4,'occ'=4] {'occ'}, dimensions={0} | all-to-all | bytes 1572864 | tf_op jit(solution)/shard_map/all_to_all | solution.py:20
  95.4 4.0 %reshape.15 = bf16[256,12,2,64]{3,2,1,0:T(2,128)(2,1)} reshape(bf16[4,2,49152]{2,1,0:T(2,128)(2,1)} %all_to_all.18) | data formatting | bytes 1572864
  99.3 3.8 %copy.13 = bf16[12,64,2,4,64]{1,3,4,0,2:T(4,128)(2,1)} copy(bf16[12,64,2,4,64]{1,2,0,4,3:T(2,128)(2,1)} %bitcast.21) | data formatting | bytes 1572864 | tf_op jit(solution)/shard_map/all_to_all | solution.py:20
  103.1 3.6 %all_to_all.16 = bf16[12,256,2,64]{1,3,0,2:T(8,128)(2,1)} reshape(bf16[12,4,64,2,64]{2,1,4,0,3:T(4,128)(2,1)} %bitcast.22) | data formatting | bytes 1572864 | tf_op jit(solution)/shard_map/all_to_all | solution.py:20
  106.7 4.3 %bitcast_convert_fusion = bf16[256,2,2048]{2,0,1:T(8,128)(2,1)} fusion(bf16[12,256,2,64]{1,3,0,2:T(8,128)(2,1)} %all_to_all.16, bf16[12,64,2048]{2,1,0:T(8,128)(2,1)S(1)} %copy-done), kind=kOutput, calls=%fused_computation | convolution fusion | flops 1611661312 | bytes 6029312 | tf_op jit(solution)/shard_map/gjwi,gip->jwp/dot_general | solution.py:22
  111.0 0.0 reduce-scatter.3.cloned.1.call-update
  111.0 0.0 reduce-scatter.5.cloned.1.call-start
  111.1 29.2 %reduce-scatter.3.cloned.1.call-done = bf16[64,2,2048]{2,0,1:T(8,128)(2,1)} async-done(((bf16[256,2,2048]{2,0,1:T(8,128)(2,1)}), bf16[64,2,2048]{2,0,1:T(8,128)(2,1)}) %reduce-scatter.3.cloned.1.call-update) | async-done | bytes 524304 | tf_op jit(solution)/shard_map/reduce_scatter | solution.py:21
  140.2 2.1 %convert_element_type.11 = f32[64,2,2048]{2,0,1:T(8,128)} convert(bf16[64,2,2048]{2,0,1:T(8,128)(2,1)} %reduce-scatter.3.cloned.1.call-done) | non-fusion elementwise | flops 262144 | bytes 1572864 | tf_op jit(solution)/shard_map/convert_element_type | solution.py:28
  142.3 0.0 reduce-scatter.5.cloned.1.call-update
  142.4 27.5 %reduce-scatter.5.cloned.1.call-done = f32[64,2,512]{2,0,1:T(8,128)} async-done(((f32[64,2,2048]{2,0,1:T(8,128)}), f32[64,2,512]{2,0,1:T(8,128)}) %reduce-scatter.5.cloned.1.call-update) | async-done | bytes 262160 | tf_op jit(solution)/shard_map/reduce_scatter | solution.py:29
  169.9 1.0 broadcast_multiply_fusion
  170.8 0.9 copy.10
Async XLA Ops:
  6.5 56.6 %copy-start = (bf16[12,64,2048]{2,1,0:T(8,128)(2,1)S(1)}, bf16[12,64,2048]{2,1,0:T(8,128)(2,1)}, u32[]{:S(2)}) copy-start(bf16[12,64,2048]{2,1,0:T(8,128)(2,1)} %param.2) | copy-start | bytes 9437188
  6.5 56.6 %all-gather.2.cloned.1.call-start = ((), (), s32[]{:S(2)}) async-start(), calls=%async_computation.3 | async-start | bytes 2621440 | tf_op jit(solution)/shard_map/all_gather | solution.py:16
  17.0 123.2 %reduce-scatter.3.cloned.1.call-start = ((), (), s32[]{:S(2)}) async-start(), calls=%async_computation.4 | async-start | bytes 2621440 | tf_op jit(solution)/shard_map/reduce_scatter | solution.py:21
  111.0 58.9 %reduce-scatter.5.cloned.1.call-start = ((), (), s32[]{:S(2)}) async-start(), calls=%async_computation.5 | async-start | bytes 1310720 | tf_op jit(solution)/shard_map/reduce_scatter | solution.py:29
Sparse Core Ops, SparseCore 0:
  17.2 45.9 all-gather.1
  111.1 29.0 reduce-scatter.2
  142.5 27.3 reduce-scatter.4
where the time goes:
time: 179 us; the launch traced here: 178 us
  waiting for transfers between devices  103 us (58%)
  blocking collectives  26.4 us (15%)
  local copies, waits for them, and re-layouts  24.2 us (14%)
  between operations  13.1 us (7%)
  matrix products  8.59 us (5%)
  other arithmetic  3.09 us (2%)
    all_gather x1, waiting for transfers between devices, local(): piece = lax.all_gather(green_all, 'chol', axis=2, tiled=True)  46.1 us
    reduce_scatter x1, waiting for transfers between devices, local(): lax.psum_scatter(jnp.einsum('gjwi,gip->jwp', swapped, chol_rot, preferred...  29.2 us
    reduce_scatter x1, waiting for transfers between devices, local(): lax.psum_scatter(occ_summed, 'chol', scatter_dimension=2, tiled=True)  27.5 us
    all_to_all x1, blocking collectives, local(): lax.all_to_all(pairs, 'occ', split_axis=3, concat_axis=1, tiled=True)  15.9 us
    all_gather x1, blocking collectives, local(): green_all = lax.all_gather(green, 'occ', axis=1, tiled=True)  10.5 us
    unnamed x4, local copies, waits for them, and re-layouts  8.02 us
    reshape x2, local copies, waits for them, and re-layouts, local(): pair_sum.astype(jnp.bfloat16).reshape(chol_loc, occ_loc, walkers, occupied)  7.95 us
    all_to_all x2, local copies, waits for them, and re-layouts, local(): lax.all_to_all(pairs, 'occ', split_axis=3, concat_axis=1, tiled=True)  7.37 us
  transfers between devices with their start and end apart: 3, of which 3 were waited for; matrix products, arithmetic and copies ran while one was open for 0% of the time, Pallas kernels for 0%

commit v1 on v0

--- a/solution.py
+++ b/solution.py
@@ -17,7 +17,10 @@
     flat = piece.reshape(-1, piece.shape[2])
     pair_sum = jnp.dot(vec_mat, flat.T, preferred_element_type=jnp.float32)
     pairs = pair_sum.astype(jnp.bfloat16).reshape(chol_loc, occ_loc, walkers, occupied)
-    swapped = lax.all_to_all(pairs, "occ", split_axis=3, concat_axis=1, tiled=True)
+    devices = lax.axis_size("occ")
+    shards = jnp.stack(jnp.split(pairs, devices, axis=3), axis=0)
+    shards = lax.all_to_all(shards, "occ", split_axis=0, concat_axis=0)
+    swapped = jnp.concatenate(shards, axis=1)
     occ_summed = lax.psum_scatter(
         jnp.einsum("gjwi,gip->jwp", swapped, chol_rot, preferred_element_type=jnp.float32).astype(
             jnp.bfloat16

time: 179 us -> 182 us (1.017)
  other arithmetic: 3.09 us -> 7.11 us
    reshape x0 -> x2, local copies, waits for them, and re-layouts: none -> 8.73 us  [local(): swapped = jnp.concatenate(shards, axis=1)]
    all_to_all x2 -> x0, local copies, waits for them, and re-layouts: 7.37 us -> none  [local(): lax.all_to_all(pairs, 'occ', split_axis=3, concat_axis=1, tiled=True)]
    reshape x2 -> x1, local copies, waits for them, and re-layouts: 7.95 us -> 2.9 us  [local(): pair_sum.astype(jnp.bfloat16).reshape(chol_loc, occ_loc, walkers, occupied)]
    another operation x0 -> x1, other arithmetic: none -> 4.01 us  [local(): shards = jnp.stack(jnp.split(pairs, devices, axis=3), axis=0)]
    another operation x0 -> x1, local copies, waits for them, and re-layouts: none -> 2.91 us  [local(): shards = jnp.stack(jnp.split(pairs, devices, axis=3), axis=0)]
where the time goes in v1:
time: 182 us
  waiting for transfers between devices  103 us (57%)
  blocking collectives  26.4 us (15%)
  local copies, waits for them, and re-layouts  23.4 us (13%)
  between operations  13.1 us (7%)
  matrix products  8.6 us (5%)
  other arithmetic  7.11 us (4%)
    all_gather x1, waiting for transfers between devices, local(): piece = lax.all_gather(green_all, 'chol', axis=2, tiled=True)  46.1 us
    reduce_scatter x1, waiting for transfers between devices, local(): lax.psum_scatter(jnp.einsum('gjwi,gip->jwp', swapped, chol_rot, preferred...  29.2 us
    reduce_scatter x1, waiting for transfers between devices, local(): lax.psum_scatter(occ_summed, 'chol', scatter_dimension=2, tiled=True)  27.5 us
    all_to_all x1, blocking collectives, local(): shards = lax.all_to_all(shards, 'occ', split_axis=0, concat_axis=0)  15.9 us
    all_gather x1, blocking collectives, local(): green_all = lax.all_gather(green, 'occ', axis=1, tiled=True)  10.5 us
    reshape x2, local copies, waits for them, and re-layouts, local(): swapped = jnp.concatenate(shards, axis=1)  8.73 us
    unnamed x4, local copies, waits for them, and re-layouts  8 us
    dot_general x1, matrix products, local(): pair_sum = jnp.dot(vec_mat, flat.T, preferred_element_type=jnp.float32)  4.3 us
  transfers between devices with their start and end apart: 3, of which 3 were waited for; matrix products, arithmetic and copies ran while one was open for 0% of the time, Pallas kernels for 0%

profile of v1, /device:TPU:0, one launch (start us, length us, event | category | flops | bytes accessed | tf_op | source)
XLA Modules:
  0.0 181.5 jit_solution(2749192723687867755)
XLA Ops:
  6.5 0.0 copy-start
  6.5 0.0 all-gather.2.cloned.1.call-start
  6.5 10.5 %all_gather.6 = bf16[2,256,512]{2,1,0:T(8,128)(2,1)} all-gather(bf16[2,64,512]{2,1,0:T(8,128)(2,1)} %param.3), channel_id=1, replica_groups=mesh['groups'=2,'chol'=4,'occ'=4] {'occ'}, dimensions={1}, use_global_device_ids=true | all-gather | bytes 655360 | tf_op jit(solution)/shard_map/all_gather | solution.py:15
  17.0 0.0 all-gather.2.cloned.1.call-update
  17.0 0.0 reduce-scatter.3.cloned.1.call-start
  17.1 46.1 %all-gather.2.cloned.1.call-done = bf16[2,256,2048]{2,1,0:T(8,128)(2,1)} async-done(((bf16[2,256,512]{2,1,0:T(8,128)(2,1)}), bf16[2,256,2048]{2,1,0:T(8,128)(2,1)}) %all-gather.2.cloned.1.call-update) | async-done | bytes 2097168 | tf_op jit(solution)/shard_map/all_gather | solution.py:16
  63.2 0.0 copy-done
  63.2 4.3 %convolution_convert_fusion = bf16[768,512]{1,0:T(8,128)(2,1)} fusion(bf16[768,2048]{1,0:T(8,128)(2,1)S(1)} %bitcast.22, bf16[512,2048]{1,0:T(8,128)(2,1)} %bitcast.24), kind=kOutput, calls=%fused_computation.3 | convolution fusion | flops 1611005952 | bytes 6029312 | tf_op jit(solution)/shard_map/dot_general | solution.py:18
  67.5 2.9 %reshape.17 = bf16[12,64,2,256]{3,2,1,0:T(2,128)(2,1)} reshape(bf16[768,512]{1,0:T(8,128)(2,1)} %convolution_convert_fusion) | data formatting | bytes 1572864 | tf_op jit(solution)/shard_map/reshape | solution.py:19
  70.4 2.9 %slice_bitcast_fusion.3 = (bf16[1,12,64,2,64]{4,3,2,1,0:T(2,128)(2,1)S(1)}, bf16[1,12,64,2,64]{4,3,2,1,0:T(2,128)(2,1)S(1)}, bf16[1,12,64,2,64]{4,3,2,1,0:T(2,128)(2,1)S(1)}, bf16[1,12,64,2,64]{4,3,2,1,0:T(2,128)(2,1)S(1)}) fusion(bf16[12,64,2,256]{3,2,1,0:T(2,128)(2,1)} %reshape.17), kind=kLoop, calls=%fused_computation.7 | loop fusion | bytes 1572864 | tf_op jit(solution)/shard_map/stack | solution.py:21
  73.3 4.0 %pad_maximum_fusion = bf16[4,12,64,2,64]{4,3,2,1,0:T(2,128)(2,1)} fusion(bf16[1,12,64,2,64]{4,3,2,1,0:T(2,128)(2,1)S(1)} %get-tuple-element.6, bf16[1,12,64,2,64]{4,3,2,1,0:T(2,128)(2,1)S(1)} %get-tuple-element.7, bf16[1,12,64,2,64]{4,3,2,1,0:T(2,128)(2,1)S(1)} %get-tuple-element.8, bf16[1,12,64,2,64]{4,3,2,1,0:T(2,128)(2,1)S(1)} %get-tuple-element.5), kind=kLoop, calls=%fused_computation.2 | loop fusion | flops 1179648 | bytes 1572864 | tf_op jit(solution)/shard_map/stack | solution.py:21
  77.3 4.0 %reshape.22 = bf16[4,2,49152]{2,1,0:T(2,128)(2,1)} reshape(bf16[4,12,64,2,64]{4,3,2,1,0:T(2,128)(2,1)} %pad_maximum_fusion) | data formatting | bytes 1572864
  81.3 15.9 %all_to_all.5 = bf16[4,2,49152]{2,1,0:T(2,128)(2,1)} all-to-all(bf16[4,2,49152]{2,1,0:T(2,128)(2,1)} %reshape.22), channel_id=1, replica_groups=mesh['groups'=2,'chol'=4,'occ'=4] {'occ'}, dimensions={0} | all-to-all | bytes 1572864 | tf_op jit(solution)/shard_map/all_to_all | solution.py:22
  97.2 4.0 %reshape.23 = bf16[4,12,64,2,64]{4,3,2,1,0:T(2,128)(2,1)} reshape(bf16[4,2,49152]{2,1,0:T(2,128)(2,1)} %all_to_all.5) | data formatting | bytes 1572864
  101.2 5.1 %copy.3 = bf16[12,4,64,2,64]{2,1,4,0,3:T(4,128)(2,1)} copy(bf16[12,4,64,2,64]{4,3,2,0,1:T(2,128)(2,1)} %bitcast.23) | data formatting | bytes 1572864 | tf_op jit(solution)/shard_map/reshape | solution.py:23
  106.3 3.6 %reshape.19 = bf16[12,256,2,64]{1,3,0,2:T(8,128)(2,1)} reshape(bf16[12,4,64,2,64]{2,1,4,0,3:T(4,128)(2,1)} %copy.3) | data formatting | bytes 1572864 | tf_op jit(solution)/shard_map/reshape | solution.py:23
  109.9 4.3 %bitcast_convert_fusion = bf16[256,2,2048]{2,0,1:T(8,128)(2,1)} fusion(bf16[12,256,2,64]{1,3,0,2:T(8,128)(2,1)} %reshape.19, bf16[12,64,2048]{2,1,0:T(8,128)(2,1)S(1)} %copy-done), kind=kOutput, calls=%fused_computation | convolution fusion | flops 1611661312 | bytes 6029312 | tf_op jit(solution)/shard_map/gjwi,gip->jwp/dot_general | solution.py:25
  114.2 0.0 reduce-scatter.3.cloned.1.call-update
  114.2 0.0 reduce-scatter.5.cloned.1.call-start
  114.3 29.2 %reduce-scatter.3.cloned.1.call-done = bf16[64,2,2048]{2,0,1:T(8,128)(2,1)} async-done(((bf16[256,2,2048]{2,0,1:T(8,128)(2,1)}), bf16[64,2,2048]{2,0,1:T(8,128)(2,1)}) %reduce-scatter.3.cloned.1.call-update) | async-done | bytes 524304 | tf_op jit(solution)/shard_map/reduce_scatter | solution.py:24
  143.5 2.1 %convert_element_type.11 = f32[64,2,2048]{2,0,1:T(8,128)} convert(bf16[64,2,2048]{2,0,1:T(8,128)(2,1)} %reduce-scatter.3.cloned.1.call-done) | non-fusion elementwise | flops 262144 | bytes 1572864 | tf_op jit(solution)/shard_map/convert_element_type | solution.py:31
  145.6 0.0 reduce-scatter.5.cloned.1.call-update
  145.6 27.5 %reduce-scatter.5.cloned.1.call-done = f32[64,2,512]{2,0,1:T(8,128)} async-done(((f32[64,2,2048]{2,0,1:T(8,128)}), f32[64,2,512]{2,0,1:T(8,128)}) %reduce-scatter.5.cloned.1.call-update) | async-done | bytes 262160 | tf_op jit(solution)/shard_map/reduce_scatter | solution.py:32
  173.1 1.0 broadcast_multiply_fusion
  174.1 0.9 copy.4
Async XLA Ops:
  6.5 56.6 %copy-start = (bf16[12,64,2048]{2,1,0:T(8,128)(2,1)S(1)}, bf16[12,64,2048]{2,1,0:T(8,128)(2,1)}, u32[]{:S(2)}) copy-start(bf16[12,64,2048]{2,1,0:T(8,128)(2,1)} %param.2) | copy-start | bytes 9437188
  6.5 56.6 %all-gather.2.cloned.1.call-start = ((), (), s32[]{:S(2)}) async-start(), calls=%async_computation.3 | async-start | bytes 2621440 | tf_op jit(solution)/shard_map/all_gather | solution.py:16
  17.0 126.4 %reduce-scatter.3.cloned.1.call-start = ((), (), s32[]{:S(2)}) async-start(), calls=%async_computation.4 | async-start | bytes 2621440 | tf_op jit(solution)/shard_map/reduce_scatter | solution.py:24
  114.2 58.9 %reduce-scatter.5.cloned.1.call-start = ((), (), s32[]{:S(2)}) async-start(), calls=%async_computation.5 | async-start | bytes 1310720 | tf_op jit(solution)/shard_map/reduce_scatter | solution.py:32
Sparse Core Ops, SparseCore 0:
  17.2 45.9 all-gather.1
  114.4 29.0 reduce-scatter.2
  145.7 27.3 reduce-scatter.4
